TPU v7x, 32 devices: a whole 2x2x4 slice. The times are simulated.
32 devices in a mesh: groups: 2 (over x), track: 4 (over y, core), frame: 4 (over z).
Axes of the slice: x: 2, y: 2, z: 4, core: 2. Of those that a mesh axis runs over, the one named last changes fastest.
Arguments:
- frames: bfloat16 [16, 4096, 256], P(('groups', 'frame')), parts along dimension 0, may hold values from -9 to 9
- query_frame: int32 [1024], P(('groups', 'track')), parts along dimension 0, may hold values from 0 to 7
- query_pixel: int32 [1024], P(('groups', 'track')), parts along dimension 0, may hold values from 0 to 4095
- cotangent: float32 [2, 16, 512], P(None, ('groups', 'frame'), 'track'), parts along dimension 1, may hold values from -48 to 48
Outputs:
- frame_grad: float32 [4096, 16, 256], P('track', ('groups', 'frame')), parts along dimension 1
- query_grad: float32 [1024, 256], P(('groups', 'track', 'frame')), parts along dimension 0
There are 2 independent parts, one for each index of `groups`. A program takes and returns all parts, laid end to end along the dimension named above; each array names one. Nothing has to cross between parts.
All inputs are finite; a program needn't handle non-finite values.
Results may differ from a plain program's by a relative error of at most 0.0029.
Values may be sent and summed in bfloat16 or wider, within the bound.
No kernel may reach another device: no remote copies, remote signals or barrier semaphores. Data moves between devices by JAX's collectives and lax.ppermute only.
A program may use at most 64 MiB of HBM per device.

v0:
```python
import jax
import jax.numpy as jnp
from jax import lax
from jax.sharding import PartitionSpec as P

C = 256
FEAT_H = 64
FEAT_W = 64


def on_device(frames, query_frame, query_pixel, cotangent):
    held_frames = frames.shape[0]
    pixels = frames.shape[1]
    channels = frames.shape[2]
    offset = lax.axis_index("frame") * held_frames
    local_index = query_frame - offset
    inside = (local_index >= 0) & (local_index < held_frames)
    row_index = jnp.clip(local_index, 0, held_frames - 1) * pixels + query_pixel
    picked = frames.reshape(held_frames * pixels, channels)[row_index]
    picked = jnp.where(inside[:, None], picked.astype(jnp.float32), 0.0)
    query_feat = lax.psum(picked.astype(jnp.bfloat16), "frame")
    score_scale = C ** (-0.5)
    pixel_ids = jnp.arange(pixels)
    coord_x = (pixel_ids % FEAT_W * (2.0 / (FEAT_W - 1)) - 1.0).astype(jnp.float32)
    coord_y = (pixel_ids // FEAT_W * (2.0 / (FEAT_H - 1)) - 1.0).astype(jnp.float32)
    scores = (
        jnp.einsum("qc,tpc->tqp", query_feat, frames, preferred_element_type=jnp.float32)
        * score_scale
    )
    peak_score = jnp.max(scores, axis=2, keepdims=True)
    exp_scores = jnp.exp(scores - peak_score)
    weights = exp_scores / jnp.sum(exp_scores, axis=2, keepdims=True)
    expect_x = jnp.sum(weights * coord_x, axis=2)
    expect_y = jnp.sum(weights * coord_y, axis=2)
    grad_x = cotangent[0]
    grad_y = cotangent[1]
    inner_sum = grad_x * expect_x + grad_y * expect_y
    cost_grad = (
        weights
        * (grad_x[:, :, None] * coord_x + grad_y[:, :, None] * coord_y - inner_sum[:, :, None])
        * score_scale
    ).astype(jnp.bfloat16)
    query_term = jnp.einsum("tqp,tpc->qc", cost_grad, frames, preferred_element_type=jnp.float32)
    query_grad = lax.psum_scatter(query_term, "frame", scatter_dimension=0, tiled=True)
    everyone = lax.all_gather(query_feat, "track", axis=0, tiled=True)
    frame_grad = jnp.einsum(
        "tqp,qc->ptc",
        lax.all_to_all(cost_grad, "track", split_axis=2, concat_axis=1, tiled=True),
        everyone,
        preferred_element_type=jnp.float32,
    )
    return (frame_grad, query_grad)


def solution(mesh):
    return jax.shard_map(
        on_device,
        mesh=mesh,
        in_specs=(
            P(("groups", "frame"), None, None),
            P(("groups", "track")),
            P(("groups", "track")),
            P(None, ("groups", "frame"), "track"),
        ),
        out_specs=(P("track", ("groups", "frame"), None), P(("groups", "track", "frame"), None)),
        check_vma=False,
    )
```

profile of v0, /device:TPU:0, one launch (start us, length us, event | category | flops | bytes accessed | tf_op | source)
XLA Modules:
  0.0 114.3 jit_solution(15682147279452416401)
XLA Ops:
  7.2 0.0 all-reduce.2.cloned.1.call-start
  7.2 0.7 compare_and_fusion
  7.9 0.7 compare_select_fusion
  8.6 3.5 %gather_fusion = bf16[128,256]{1,0:T(8,128)(2,1)S(1)} fusion(bf16[8192,256]{1,0:T(8,128)(2,1)} %bitcast.38, s32[1024]{0:T(1024)S(1)} %pad_clamp_fusion), kind=kCustom, calls=%fused_computation | custom fusion | bytes 131584 | tf_op jit(solution)/shard_map/gather | solution.py:19
  12.1 0.7 select_convert_fusion
  12.8 0.0 all-reduce.2.cloned.1.call-update
  12.8 0.7 slice_bitcast_fusion.1
  13.5 36.5 %all-reduce.2.cloned.1.call-done = bf16[128,256]{1,0:T(8,128)(2,1)} async-done(((bf16[128,256]{1,0:T(8,128)(2,1)}), bf16[128,256]{1,0:T(8,128)(2,1)}) %all-reduce.2.cloned.1.call-update) | async-done | bytes 65552 | tf_op jit(solution)/shard_map/psum | solution.py:21
  50.0 0.0 copy-start.1
  50.0 7.0 %multiply_reduce_fusion.1 = (f32[2,128]{1,0:T(2,128)S(1)}, f32[2,128]{1,0:T(2,128)S(1)}, f32[2,128,4096]{2,1,0:T(8,128)}) fusion(f32[4096]{0:T(1024)S(1)} %get-tuple-element.11, f32[4096]{0:T(1024)S(1)} %get-tuple-element.12, bf16[2,4096,256]{2,1,0:T(8,128)(2,1)} %param.4, bf16[128,256]{1,0:T(8,128)(2,1)} %all-reduce.2.cloned.1.call-done), kind=kOutput, calls=%fused_computation.10 | convolution fusion | flops 544219136 | bytes 8488960 | tf_op jit(solution)/shard_map/div | solution.py:32
  57.0 0.0 copy-done.1
  57.0 3.5 %multiply_convert_fusion = bf16[2,128,4096]{2,1,0:T(8,128)(2,1)S(1)} fusion(f32[2,128,4096]{2,1,0:T(8,128)} %get-tuple-element.10, f32[2,128]{1,0:T(2,128)S(1)} %multiply_add_fusion, f32[4096]{0:T(1024)S(1)} %get-tuple-element.12, f32[2,128]{1,0:T(2,128)S(1)} %get-tuple-element.9, f32[4096]{0:T(1024)S(1)} %get-tuple-element.11, f32[2,128]{1,0:T(2,128)S(1)} %get-tuple-element.8), kind=kLoop, calls=%fused_computation.8 | loop fusion | flops 7340032 | bytes 6327296 | tf_op jit(solution)/shard_map/convert_element_type | solution.py:42
  60.5 3.8 %copy.9 = bf16[2,128,4096]{1,0,2:T(2,128)(2,1)} copy(bf16[2,128,4096]{2,1,0:T(8,128)(2,1)S(1)} %multiply_convert_fusion) | data formatting | bytes 4194304 | tf_op jit(solution)/shard_map/convert_element_type | solution.py:42
  64.2 4.4 %all-to-all-start = ((bf16[2,128,4096]{1,0,2:T(2,128)(2,1)}), bf16[2,128,4096]{1,0,2:T(2,128)(2,1)}, u32[]{:S(2)}, u32[]{:S(2)}) async-start(bf16[2,128,4096]{1,0,2:T(2,128)(2,1)} %copy.9), calls=%async_computation | async-start | bytes 4194304 | tf_op jit(solution)/shard_map/all_to_all | solution.py:48
  68.7 0.0 copy-start
  68.7 0.0 reduce-scatter.2.cloned.1.call-start
  68.7 3.6 %convolution_bitcast_fusion.1 = f32[128,256]{1,0:T(8,128)} fusion(bf16[2,128,4096]{2,1,0:T(8,128)(2,1)S(1)} %multiply_convert_fusion, bf16[2,4096,256]{2,1,0:T(8,128)(2,1)} %param.4), kind=kOutput, calls=%fused_computation.12 | convolution fusion | flops 536870912 | bytes 6422528 | tf_op jit(solution)/shard_map/tqp,tpc->qc/dot_general | solution.py:43
  72.3 0.0 reduce-scatter.2.cloned.1.call-update
  72.3 0.0 copy-done
  72.3 24.2 %all_gather.3 = bf16[512,256]{1,0:T(8,128)(2,1)S(1)} all-gather(bf16[128,256]{1,0:T(8,128)(2,1)S(1)} %copy-done), channel_id=1, replica_groups=mesh['groups'=2,'track'=4,'frame'=4] {'track'}, dimensions={0}, use_global_device_ids=true | all-gather | bytes 327680 | tf_op jit(solution)/shard_map/all_gather | solution.py:45
  96.6 0.0 all-to-all-done
  96.6 4.7 %copy.10 = bf16[2,128,4,1024]{3,1,2,0:T(8,128)(2,1)S(1)} copy(bf16[2,128,4,1024]{1,0,3,2:T(2,128)(2,1)} %bitcast.6) | data formatting | bytes 4194304 | tf_op jit(solution)/shard_map/all_to_all | solution.py:48
  101.3 2.1 %convolution_bitcast_fusion = f32[1024,2,256]{0,2,1:T(8,128)} fusion(bf16[2,512,1024]{2,1,0:T(8,128)(2,1)S(1)} %bitcast.37, bf16[512,256]{1,0:T(8,128)(2,1)S(1)} %all_gather.3), kind=kOutput, calls=%fused_computation.11 | convolution fusion | flops 536870912 | bytes 4456448 | tf_op jit(solution)/shard_map/tqp,qc->ptc/dot_general | solution.py:46
  103.4 4.1 %copy.12 = f32[1024,2,256]{2,1,0:T(2,128)} copy(f32[1024,2,256]{0,2,1:T(8,128)} %convolution_bitcast_fusion) | data formatting | bytes 4194304
  107.5 0.0 reduce-scatter.2.cloned.1.call-done
  (3 shorter events, 0.0 us)
Async XLA Ops:
  7.2 42.8 %all-reduce.2.cloned.1.call-start = ((), (), s32[]{:S(2)}) async-start(), calls=%async_computation.2 | async-start | bytes 131072 | tf_op jit(solution)/shard_map/psum | solution.py:21
  50.0 7.0 %copy-start.1 = (f32[2,2,128]{2,1,0:T(2,128)S(1)}, f32[2,2,128]{2,1,0:T(2,128)}, u32[]{:S(2)}) copy-start(f32[2,2,128]{2,1,0:T(2,128)} %param.7) | copy-start | bytes 6148
  64.2 32.3 %all-to-all-start = ((bf16[2,128,4096]{1,0,2:T(2,128)(2,1)}), bf16[2,128,4096]{1,0,2:T(2,128)(2,1)}, u32[]{:S(2)}, u32[]{:S(2)}) async-start(bf16[2,128,4096]{1,0,2:T(2,128)(2,1)} %copy.9), calls=%async_computation | async-start | bytes 4194304 | tf_op jit(solution)/shard_map/all_to_all | solution.py:48
  68.7 3.6 %copy-start = (bf16[128,256]{1,0:T(8,128)(2,1)S(1)}, bf16[128,256]{1,0:T(8,128)(2,1)}, u32[]{:S(2)}) copy-start(bf16[128,256]{1,0:T(8,128)(2,1)} %all-reduce.2.cloned.1.call-done) | copy-start | bytes 196612
  68.7 38.8 %reduce-scatter.2.cloned.1.call-start = ((), (), s32[]{:S(2)}) async-start(), calls=%async_computation.3 | async-start | bytes 163840 | tf_op jit(solution)/shard_map/reduce_scatter | solution.py:44
Sparse Core Ops, SparseCore 0:
  12.9 37.0 all-reduce.1
  72.4 19.6 reduce-scatter.1
where the time goes:
time: 115 us; the launch traced here: 114 us
  waiting for transfers between devices  36.5 us (32%)
  blocking collectives  24.2 us (21%)
  local copies, waits for them, and re-layouts  16.8 us (15%)
  between operations  14.1 us (12%)
  matrix products  12.7 us (11%)
  other arithmetic  5.55 us (5%)
  starting transfers between devices  4.52 us (4%)
    psum x1, waiting for transfers between devices, on_device(): query_feat = lax.psum(picked.astype(jnp.bfloat16), 'frame')  36.5 us
    all_gather x1, blocking collectives, on_device(): everyone = lax.all_gather(query_feat, 'track', axis=0, tiled=True)  24.2 us
    div x1, matrix products, on_device(): weights = exp_scores / jnp.sum(exp_scores, axis=2, keepdims=True)  7.01 us
    all_to_all x1, local copies, waits for them, and re-layouts, on_device(): lax.all_to_all(cost_grad, 'track', split_axis=2, concat_axis=1, tiled=True)  4.73 us
    all_to_all x1, starting transfers between devices, on_device(): lax.all_to_all(cost_grad, 'track', split_axis=2, concat_axis=1, tiled=True)  4.44 us
    unnamed x5, local copies, waits for them, and re-layouts  4.12 us
    convert_element_type x1, local copies, waits for them, and re-layouts, on_device(): cost_grad = (weights * (grad_x[:, :, None] * coord_x + grad_y[:, :, None]...  3.77 us
    dot_general x1, matrix products, on_device(): jnp.einsum('tqp,tpc->qc', cost_grad, frames, preferred_element_type=jnp.f...  3.56 us
  transfers between devices with their start and end apart: 3, of which 1 were waited for; matrix products, arithmetic and copies ran while one was open for 13% of the time, Pallas kernels for 0%

commit v1 on v0

v1 whole, which is shorter than its diff:
```python
import functools
import math

import jax
import jax.numpy as jnp
from jax import lax
from jax.experimental import pallas as pl
from jax.experimental.pallas import tpu as pltpu
from jax.sharding import PartitionSpec as P

C = 256
FEAT_H = 64
FEAT_W = 64
LANES = 128
LOG2E = math.log2(math.e)
F32 = jnp.float32
BF16 = jnp.bfloat16

COPY_ROWS = 1024
PICK_COLS = 1024
SCORE_COLS = 512
BLOCK_ROWS = 32
NT = (((1,), (1,)), ((), ()))
VMEM_SPEC = pl.BlockSpec(memory_space=pltpu.VMEM)
HBM_SPEC = pl.BlockSpec(memory_space=pltpu.HBM)
SMEM_SPEC = pl.BlockSpec(memory_space=pltpu.SMEM)
PARAMS = pltpu.CompilerParams(vmem_limit_bytes=40 << 20)


def xor_permute(value, axis, size, distance):
    return lax.ppermute(value, axis, [(i, i ^ distance) for i in range(size)])


def column_tile(row):
    return jnp.transpose(jnp.broadcast_to(row, (LANES, row.shape[1])))


def pick_kernel(held, pixels, place, frame_ref, pixel_ref, frames_hbm, frames_out, picked_ref, sems):
    rows = held * pixels
    count = rows // COPY_ROWS
    copies = [
        pltpu.make_async_copy(
            frames_hbm.at[pl.ds(i * COPY_ROWS, COPY_ROWS), :],
            frames_out.at[pl.ds(i * COPY_ROWS, COPY_ROWS), :],
            sems.at[i],
        )
        for i in range(count)
    ]
    for copy in copies:
        copy.start()
    local = frame_ref[...] - place[0] * held
    inside = (local >= 0) & (local < held)
    index = jnp.where(inside, local * pixels + pixel_ref[...], -1)
    tracks = index.shape[1]
    column = column_tile(index)
    lane = lax.broadcasted_iota(jnp.int32, (tracks, LANES), 1)
    total = jnp.zeros((tracks, picked_ref.shape[1]), F32)
    for i, copy in enumerate(copies):
        copy.wait()
        for start in range(i * COPY_ROWS, (i + 1) * COPY_ROWS, PICK_COLS):
            hits = [
                jnp.where(column - (start + at) == lane, 1.0, 0.0).astype(BF16)
                for at in range(0, PICK_COLS, LANES)
            ]
            total += jnp.dot(
                jnp.concatenate(hits, axis=1),
                frames_out[pl.ds(start, PICK_COLS), :],
                preferred_element_type=F32,
            )
    picked_ref[...] = total.astype(BF16)


def track_kernel(held, pixels, place, parts, feat_ref, frames_ref, cot_ref, stats_ref, *rest):
    part_refs, scores, term = rest[: parts], rest[parts], rest[parts + 1]
    tracks = feat_ref.shape[0]
    scale = C ** (-0.5)
    lane = lax.broadcasted_iota(jnp.int32, (1, LANES), 1)
    rows_per_tile = LANES // FEAT_W
    lane_x = (lane % FEAT_W).astype(F32) * (2.0 / (FEAT_W - 1)) - 1.0
    lane_y = (lane // FEAT_W).astype(F32) * (2.0 / (FEAT_H - 1)) - 1.0
    step_y = rows_per_tile * (2.0 / (FEAT_H - 1))
    feat = feat_ref[...]
    total = jnp.zeros(term.shape, F32)
    stat_rows = []
    for t in range(held):
        base = t * pixels
        peak = jnp.full((tracks, LANES), -jnp.inf, F32)
        for start in range(0, pixels, SCORE_COLS):
            block = lax.dot_general(
                feat, frames_ref[pl.ds(base + start, SCORE_COLS), :], NT, preferred_element_type=F32
            ) * (scale * LOG2E)
            scores[:, pl.ds(base + start, SCORE_COLS)] = block
            for at in range(0, SCORE_COLS, LANES):
                peak = jnp.maximum(peak, block[:, at : at + LANES])
        peak = jnp.broadcast_to(jnp.max(peak, axis=1, keepdims=True), (tracks, LANES))
        grad_x = column_tile(cot_ref[0, pl.ds(t, 1), :])
        grad_y = column_tile(cot_ref[1, pl.ds(t, 1), :])
        coefs = []
        for first in range(0, tracks, BLOCK_ROWS):
            lines = pl.ds(first, BLOCK_ROWS)
            top = peak[first : first + BLOCK_ROWS]
            sums = jnp.zeros((BLOCK_ROWS, LANES), F32)
            sums_y = jnp.zeros((BLOCK_ROWS, LANES), F32)
            for tile in range(pixels // LANES):
                cols = pl.ds(base + tile * LANES, LANES)
                power = jnp.exp2(scores[lines, cols] - top)
                scores[lines, cols] = power
                sums += power
                sums_y += power * (tile * step_y)
            norm = jnp.sum(sums, axis=1, keepdims=True)
            inverse = 1.0 / norm
            expect_x = jnp.sum(sums * lane_x, axis=1, keepdims=True) * inverse
            expect_y = jnp.sum(sums_y + sums * lane_y, axis=1, keepdims=True) * inverse
            gx = grad_x[first : first + BLOCK_ROWS]
            gy = grad_y[first : first + BLOCK_ROWS]
            factor = inverse * scale
            inner = (gx * expect_x + gy * expect_y) * factor
            gx = gx * factor
            gy = gy * factor
            coefs.append((gx, gy, inner))
        gx, gy, inner = (jnp.concatenate(list(c), axis=0) for c in zip(*coefs))
        table = gx * lane_x + gy * lane_y - inner
        for value in (peak, gx, gy, inner):
            stat_rows.append(jnp.transpose(value)[0:1])
        for start in range(0, pixels, SCORE_COLS):
            grads = []
            for at in range(start, start + SCORE_COLS, LANES):
                power = scores[:, pl.ds(base + at, LANES)]
                grads.append((power * (table + gy * ((at // LANES) * step_y))).astype(BF16))
            total += jnp.dot(
                jnp.concatenate(grads, axis=1),
                frames_ref[pl.ds(base + start, SCORE_COLS), :],
                preferred_element_type=F32,
            )
    stats_ref[...] = jnp.concatenate(stat_rows, axis=0)
    term[...] = total
    share = tracks // parts
    for i, part in enumerate(part_refs):
        owner = place[0] ^ i
        part[...] = term[pl.ds(pl.multiple_of(owner * share, share), share), :]


def frame_kernel(held, pixels, blocks, place, *refs):
    feat_refs, stat_refs = refs[:blocks], refs[blocks : 2 * blocks]
    frames_ref, out_ref = refs[2 * blocks], refs[2 * blocks + 1]
    scale = C ** (-0.5)
    own = out_ref.shape[0] // (held * (C // LANES))
    start_row = place[1] * own
    image_row0 = (start_row // FEAT_W).astype(F32)
    line_x = (lax.broadcasted_iota(jnp.int32, (FEAT_W, LANES), 0)).astype(F32) * (2.0 / (FEAT_W - 1)) - 1.0
    feats = [ref[...] for ref in feat_refs]
    tracks = feats[0].shape[0]
    everyone = jnp.concatenate(feats, axis=0)
    chunk = min(own, 256)
    for t in range(held):
        tables, peaks, slopes, inners = [], [], [], []
        for ref in stat_refs:
            for at in range(0, tracks, LANES):
                row = lambda k: ref[pl.ds(4 * t + k, 1), pl.ds(at, LANES)]
                peaks.append(row(0))
                tables.append(row(1) * line_x)
                slopes.append(row(2))
                inners.append(row(3))
        for first in range(0, own, chunk):
            lines = frames_ref[pl.ds(pl.multiple_of(t * pixels + start_row + first, FEAT_W), chunk), :]
            score = lax.dot_general(lines, everyone, NT, preferred_element_type=F32) * (scale * LOG2E)
            images = []
            for image in range(chunk // FEAT_W):
                coord_y = (image_row0 + (first // FEAT_W + image)) * (2.0 / (FEAT_H - 1)) - 1.0
                grads = []
                for b in range(len(peaks)):
                    part = score[image * FEAT_W : (image + 1) * FEAT_W, b * LANES : (b + 1) * LANES]
                    power = jnp.exp2(part - peaks[b])
                    grads.append((power * (tables[b] + (slopes[b] * coord_y - inners[b]))).astype(BF16))
                images.append(jnp.concatenate(grads, axis=1))
            grad = jnp.concatenate(images, axis=0)
            value = jnp.dot(grad, everyone, preferred_element_type=F32)
            lanes_tiles = C // LANES
            for k in range(lanes_tiles):
                out_ref[pl.ds(first * held * lanes_tiles + k * held + t, chunk, stride=held * lanes_tiles), :] = value[
                    :, k * LANES : (k + 1) * LANES
                ]


def on_device(sizes, frames, query_frame, query_pixel, cotangent):
    ranks, columns = sizes["frame"], sizes["track"]
    held, pixels, channels = frames.shape
    tracks = query_frame.shape[0]
    place = jnp.stack([lax.axis_index("frame"), lax.axis_index("track")]).astype(jnp.int32)
    flat = pltpu.with_memory_space_constraint(frames.reshape(held * pixels, channels), pltpu.HBM)

    kept, feat = pl.pallas_call(
        functools.partial(pick_kernel, held, pixels),
        out_shape=(pltpu.VMEM((held * pixels, channels), BF16), pltpu.VMEM((tracks, channels), BF16)),
        in_specs=[SMEM_SPEC, VMEM_SPEC, VMEM_SPEC, HBM_SPEC],
        out_specs=(VMEM_SPEC, VMEM_SPEC),
        scratch_shapes=[pltpu.SemaphoreType.DMA((held * pixels // COPY_ROWS,))],
        compiler_params=PARAMS,
        name="pick",
    )(place, query_frame[None], query_pixel[None], flat)

    distance = 1
    while distance < ranks:
        feat = feat + xor_permute(feat, "frame", ranks, distance)
        distance *= 2

    share = tracks // ranks
    stats, *terms = pl.pallas_call(
        lambda place_ref, *refs: track_kernel(held, pixels, place_ref, ranks, *refs),
        out_shape=(pltpu.VMEM((4 * held, tracks), F32),)
        + tuple(pltpu.VMEM((share, channels), F32) for _ in range(ranks)),
        in_specs=[SMEM_SPEC, VMEM_SPEC, VMEM_SPEC, VMEM_SPEC],
        out_specs=(VMEM_SPEC,) * (1 + ranks),
        scratch_shapes=[pltpu.VMEM((tracks, held * pixels), F32), pltpu.VMEM((tracks, channels), F32)],
        compiler_params=PARAMS,
        name="own_tracks",
    )(place, feat, kept, cotangent)

    feats, all_stats = [feat], [stats]
    for step in range(1, columns):
        feats.append(xor_permute(feat, "track", columns, step))
        all_stats.append(xor_permute(stats, "track", columns, step))
    query_grad = terms[0]
    arrived = [xor_permute(terms[i], "frame", ranks, i) for i in range(1, ranks)]

    own = pixels // columns
    frame_grad = pl.pallas_call(
        lambda place_ref, *refs: frame_kernel(held, pixels, columns, place_ref, *refs),
        out_shape=jax.ShapeDtypeStruct((own * held * channels // LANES, LANES), F32),
        in_specs=[SMEM_SPEC] + [VMEM_SPEC] * (2 * columns + 1),
        out_specs=VMEM_SPEC,
        compiler_params=PARAMS,
        cost_estimate=pl.CostEstimate(
            flops=4 * held * own * tracks * columns * channels,
            bytes_accessed=4 * held * own * channels,
            transcendentals=held * own * tracks * columns,
        ),
        name="own_pixels",
    )(place, *feats, *all_stats, kept)
    frame_grad = frame_grad.reshape(own, channels // LANES, held, LANES)
    frame_grad = jnp.transpose(frame_grad, (0, 2, 1, 3)).reshape(own, held, channels)
    for value in arrived:
        query_grad = query_grad + value
    return (frame_grad, query_grad)


def solution(mesh):
    return jax.shard_map(
        functools.partial(on_device, dict(mesh.shape)),
        mesh=mesh,
        in_specs=(
            P(("groups", "frame"), None, None),
            P(("groups", "track")),
            P(("groups", "track")),
            P(None, ("groups", "frame"), "track"),
        ),
        out_specs=(P("track", ("groups", "frame"), None), P(("groups", "track", "frame"), None)),
        check_vma=False,
    )
```

time: 115 us -> 38.3 us (0.33)
  waiting for transfers between devices: 36.5 us -> 8.48 us
  blocking collectives: 24.2 us -> 0 us
  local copies, waits for them, and re-layouts: 16.8 us -> 1.31 us
  between operations: 14.1 us -> 0.69 us
  matrix products: 12.7 us -> 0 us
  starting transfers between devices: 4.52 us -> 15.8 us
  Pallas kernels: 0 us -> 11.1 us
  other arithmetic: 5.55 us -> 0.74 us
    psum x1 -> x0, waiting for transfers between devices: 36.5 us -> none  [on_device(): query_feat = lax.psum(picked.astype(jnp.bfloat16), 'frame')]
    all_gather x1 -> x0, blocking collectives: 24.2 us -> none  [on_device(): everyone = lax.all_gather(query_feat, 'track', axis=0, tiled=True)]
    ppermute x0 -> x11, starting transfers between devices: none -> 15.8 us  [xor_permute(): return lax.ppermute(value, axis, [(i, i ^ distance) for i in range(size)])]
    pallas_call x0 -> x3, Pallas kernels: none -> 11.1 us  [the longest x1 4.5 us: on_device(): pl.pallas_call(lambda place_ref, *refs: track_kernel(held, pixels, place_...]
    ppermute x0 -> x11, waiting for transfers between devices: none -> 8.48 us  [xor_permute(): return lax.ppermute(value, axis, [(i, i ^ distance) for i in range(size)])]
    div x1 -> x0, matrix products: 7.01 us -> none  [on_device(): weights = exp_scores / jnp.sum(exp_scores, axis=2, keepdims=True)]
    dot_general x2 -> x0, matrix products: 5.64 us -> none  [the longest x1 3.56 us: on_device(): jnp.einsum('tqp,tpc->qc', cost_grad, frames, preferred_element_type=jnp.f...]
    all_to_all x1 -> x0, local copies, waits for them, and re-layouts: 4.73 us -> none  [on_device(): lax.all_to_all(cost_grad, 'track', split_axis=2, concat_axis=1, tiled=True)]
  transfers between devices with their start and end apart: 3 -> 11, of which waited for: 1 -> 5; matrix products, arithmetic and copies ran while one was open for 13% -> 2% of each run, Pallas kernels for 0% -> 0%
where the time goes in v1:
time: 38.3 us; the launch traced here: 38.1 us
  starting transfers between devices  15.8 us (41%)
  Pallas kernels  11.1 us (29%)
  waiting for transfers between devices  8.48 us (22%)
  local copies, waits for them, and re-layouts  1.31 us (3%)
  other arithmetic  0.74 us (2%)
  between operations  0.69 us (2%)
    ppermute x11, starting transfers between devices, xor_permute(): return lax.ppermute(value, axis, [(i, i ^ distance) for i in range(size)])  15.8 us
    ppermute x11, waiting for transfers between devices, xor_permute(): return lax.ppermute(value, axis, [(i, i ^ distance) for i in range(size)])  8.48 us
    pallas_call x1, Pallas kernels, on_device(): pl.pallas_call(lambda place_ref, *refs: track_kernel(held, pixels, place_...  4.5 us
    pallas_call x1, Pallas kernels, on_device(): pl.pallas_call(functools.partial(pick_kernel, held, pixels), out_shape=(p...  3.36 us
    pallas_call x1, Pallas kernels, on_device(): pl.pallas_call(lambda place_ref, *refs: frame_kernel(held, pixels, column...  3.27 us
    unnamed x6, local copies, waits for them, and re-layouts  1.31 us
  transfers between devices with their start and end apart: 11, of which 5 were waited for; matrix products, arithmetic and copies ran while one was open for 2% of the time, Pallas kernels for 0%

profile of v1, /device:TPU:0, one launch (start us, length us, event | category | flops | bytes accessed | tf_op | source)
XLA Modules:
  0.0 38.1 jit_solution(9557262448878281453)
XLA Ops:
  0.6 0.0 copy-start
  0.6 0.1 pad_add_fusion.place.place_ref
  0.7 0.0 copy-start.1
  0.7 0.7 %copy-done.1 = s32[128]{0:T(128)S(1)} copy-done((s32[128]{0:T(128)S(1)}, s32[128]{0:T(128)}, u32[]{:S(2)}) %copy-start.1) | copy-done | bytes 536
  1.4 0.0 copy-start.2
  1.4 0.7 %copy-done.2 = s32[128]{0:T(128)S(1)} copy-done((s32[128]{0:T(128)S(1)}, s32[128]{0:T(128)}, u32[]{:S(2)}) %copy-start.2) | copy-done | bytes 536
  2.0 3.4 %pick.1 = (bf16[8192,256]{1,0:T(8,128)(2,1)S(1)}, bf16[128,256]{1,0:T(8,128)(2,1)S(1)}) custom-call(s32[2]{0:T(128)S(1)} %pad_add_fusion.place.place_ref, s32[1,128]{1,0:T(1,128)S(1)} %bitcast.10, s32[1,128]{1,0:T(1,128)S(1)} %bitcast.11, bf16[8192,256]{1,0:T(8,128)(2,1)} %bitcast.12), custom_call_target="tpu_custom_call" | custom-call | tf_op jit(solution)/shard_map/pick/pallas_call | solution.py:192
  5.4 3.1 %collective-permute-start = (bf16[128,256]{1,0:T(8,128)(2,1)S(1)}, bf16[128,256]{1,0:T(8,128)(2,1)S(1)}, u32[]{:S(2)}, u32[]{:S(2)}) collective-permute-start(bf16[128,256]{1,0:T(8,128)(2,1)S(1)} %get-tuple-element.9), channel_id=1, source_target_pairs={{0,1},{1,0},{2,3},{3,2},{4,5},{5,4},{6,7},{7,6},{8,9},{9,8},{10,11... | collective-permute-start | bytes 196616 | tf_op jit(solution)/shard_map/ppermute | solution.py:31
  8.5 2.2 %collective-permute-done = bf16[128,256]{1,0:T(8,128)(2,1)S(1)} collective-permute-done((bf16[128,256]{1,0:T(8,128)(2,1)S(1)}, bf16[128,256]{1,0:T(8,128)(2,1)S(1)}, u32[]{:S(2)}, u32[]{:S(2)}) %collective-permute-start) | collective-permute-done | bytes 65568 | tf_op jit(solution)/shard_map/ppermute | solution.py:31
  10.8 3.1 %collective-permute-start.1 = (bf16[128,256]{1,0:T(8,128)(2,1)S(1)}, bf16[128,256]{1,0:T(8,128)(2,1)S(1)}, u32[]{:S(2)}, u32[]{:S(2)}) collective-permute-start(bf16[128,256]{1,0:T(8,128)(2,1)S(1)} %add.15), channel_id=1, source_target_pairs={{0,2},{1,3},{2,0},{3,1},{4,6},{5,7},{6,4},{7,5},{8,10},{9,11},{10,... | collective-permute-start | bytes 196616 | tf_op jit(solution)/shard_map/ppermute | solution.py:31
  13.9 2.2 %collective-permute-done.1 = bf16[128,256]{1,0:T(8,128)(2,1)S(1)} collective-permute-done((bf16[128,256]{1,0:T(8,128)(2,1)S(1)}, bf16[128,256]{1,0:T(8,128)(2,1)S(1)}, u32[]{:S(2)}, u32[]{:S(2)}) %collective-permute-start.1) | collective-permute-done | bytes 65568 | tf_op jit(solution)/shard_map/ppermute | solution.py:31
  16.2 0.0 copy-done
  16.2 4.5 %own_tracks.1 = (f32[8,128]{1,0:T(8,128)S(1)}, f32[32,256]{1,0:T(8,128)S(1)}, f32[32,256]{1,0:T(8,128)S(1)}, f32[32,256]{1,0:T(8,128)S(1)}, f32[32,256]{1,0:T(8,128)S(1)}) custom-call(s32[2]{0:T(128)S(1)} %pad_add_fusion.place.place_ref, bf16[128,256]{1,0:T(8,128)(2,1)S(1)} %add.16.refs_0_, bf16[8192,256]{1,0:T(8,128)(2,1)S(1)} %get-tuple-element.10.refs_1_.refs_8_, ...), custom_call_target="tpu_custom_call" | custom-call | tf_op jit(solution)/shard_map/own_tracks/pallas_call | solution.py:208
  20.7 4.6 %collective-permute-start.10 = (f32[32,256]{1,0:T(8,128)S(1)}, f32[32,256]{1,0:T(8,128)S(1)}, u32[]{:S(2)}, u32[]{:S(2)}) collective-permute-start(f32[32,256]{1,0:T(8,128)S(1)} %get-tuple-element.15), channel_id=1, source_target_pairs={{0,3},{1,2},{2,1},{3,0},{4,7},{5,6},{6,5},{7,4},{8,11},{9,10},{10,... | collective-permute-start | bytes 98312 | tf_op jit(solution)/shard_map/ppermute | solution.py:31
  25.3 0.0 collective-permute-start.8
  25.3 0.6 %collective-permute-start.9 = (f32[32,256]{1,0:T(8,128)S(1)}, f32[32,256]{1,0:T(8,128)S(1)}, u32[]{:S(2)}, u32[]{:S(2)}) collective-permute-start(f32[32,256]{1,0:T(8,128)S(1)} %get-tuple-element.14), channel_id=1, source_target_pairs={{0,2},{1,3},{2,0},{3,1},{4,6},{5,7},{6,4},{7,5},{8,10},{9,11},{10,... | collective-permute-start | bytes 98312 | tf_op jit(solution)/shard_map/ppermute | solution.py:31
  25.9 0.0 collective-permute-start.5
  25.9 1.5 %collective-permute-start.6 = (f32[8,128]{1,0:T(8,128)S(1)}, f32[8,128]{1,0:T(8,128)S(1)}, u32[]{:S(2)}, u32[]{:S(2)}) collective-permute-start(f32[8,128]{1,0:T(8,128)S(1)} %get-tuple-element.11.refs_4_), channel_id=1, source_target_pairs={{0,8},{4,12},{8,0},{12,4},{1,9},{5,13},{9,1},{13,5},{2,10},{6,14},... | collective-permute-start | bytes 12296 | tf_op jit(solution)/shard_map/ppermute | solution.py:31
  27.4 0.0 collective-permute-done.5.refs_5_
  27.4 0.9 %collective-permute-start.7 = (f32[8,128]{1,0:T(8,128)S(1)}, f32[8,128]{1,0:T(8,128)S(1)}, u32[]{:S(2)}, u32[]{:S(2)}) collective-permute-start(f32[8,128]{1,0:T(8,128)S(1)} %get-tuple-element.11.refs_4_), channel_id=1, source_target_pairs={{0,12},{4,8},{8,4},{12,0},{1,13},{5,9},{9,5},{13,1},{2,14},{6,10},... | collective-permute-start | bytes 12296 | tf_op jit(solution)/shard_map/ppermute | solution.py:31
  28.4 0.0 collective-permute-done.10
  28.4 0.3 collective-permute-start.2
  28.7 0.5 %collective-permute-done.8 = f32[32,256]{1,0:T(8,128)S(1)} collective-permute-done((f32[32,256]{1,0:T(8,128)S(1)}, f32[32,256]{1,0:T(8,128)S(1)}, u32[]{:S(2)}, u32[]{:S(2)}) %collective-permute-start.8) | collective-permute-done | bytes 32800 | tf_op jit(solution)/shard_map/ppermute | solution.py:31
  29.2 1.5 %collective-permute-start.3 = (bf16[128,256]{1,0:T(8,128)(2,1)S(1)}, bf16[128,256]{1,0:T(8,128)(2,1)S(1)}, u32[]{:S(2)}, u32[]{:S(2)}) collective-permute-start(bf16[128,256]{1,0:T(8,128)(2,1)S(1)} %add.16.refs_0_), channel_id=1, source_target_pairs={{0,8},{4,12},{8,0},{12,4},{1,9},{5,13},{9,1},{13,5},{2,10},{6,14},... | collective-permute-start | bytes 196616 | tf_op jit(solution)/shard_map/ppermute | solution.py:31
  30.7 0.0 collective-permute-done.9
  30.7 0.0 collective-permute-start.4
  30.7 0.6 %add_add_fusion = f32[32,256]{1,0:T(8,128)} fusion(f32[32,256]{1,0:T(8,128)S(1)} %collective-permute-done.10, f32[32,256]{1,0:T(8,128)S(1)} %collective-permute-done.9, f32[32,256]{1,0:T(8,128)S(1)} %get-tuple-element.12, f32[32,256]{1,0:T(8,128)S(1)} %collective-permute-done.8), kind=kLoop, calls=%fused_computation | loop fusion | flops 24576 | bytes 163840 | tf_op jit(solution)/shard_map/add | solution.py:243
  31.3 0.0 collective-permute-done.6.refs_6_
  31.3 0.0 collective-permute-done.7.refs_7_
  31.3 0.0 collective-permute-done.2.refs_1_
  31.3 2.1 %collective-permute-done.3.refs_2_ = bf16[128,256]{1,0:T(8,128)(2,1)S(1)} collective-permute-done((bf16[128,256]{1,0:T(8,128)(2,1)S(1)}, bf16[128,256]{1,0:T(8,128)(2,1)S(1)}, u32[]{:S(2)}, u32[]{:S(2)}) %collective-permute-start.3) | collective-permute-done | bytes 65568 | tf_op jit(solution)/shard_map/ppermute | solution.py:31
  33.4 1.4 %collective-permute-done.4.refs_3_ = bf16[128,256]{1,0:T(8,128)(2,1)S(1)} collective-permute-done((bf16[128,256]{1,0:T(8,128)(2,1)S(1)}, bf16[128,256]{1,0:T(8,128)(2,1)S(1)}, u32[]{:S(2)}, u32[]{:S(2)}) %collective-permute-start.4) | collective-permute-done | bytes 65568 | tf_op jit(solution)/shard_map/ppermute | solution.py:31
  34.8 3.3 %own_pixels.1 = f32[4096,128]{1,0:T(8,128)} custom-call(s32[2]{0:T(128)S(1)} %pad_add_fusion.place.place_ref, bf16[128,256]{1,0:T(8,128)(2,1)S(1)} %add.16.refs_0_, bf16[128,256]{1,0:T(8,128)(2,1)S(1)} %collective-permute-done.2.refs_1_, bf16[128,256]{1,0:T(8,128)(2,1)S(1)} %collective-permute-done.3.refs_2_, ...), custom_call_target="tpu_custom_call" | custom-call | flops 1073741824 | bytes 2097152 | tf_op jit(solution)/shard_map/own_pixels/pallas_call | solution.py:227
  (2 shorter events, 0.0 us)
Async XLA Ops:
  0.6 15.5 %copy-start = (f32[2,2,128]{2,1,0:T(2,128)S(1)}, f32[2,2,128]{2,1,0:T(2,128)}, u32[]{:S(2)}) copy-start(f32[2,2,128]{2,1,0:T(2,128)} %refs_2_.1) | copy-start | bytes 6148
  0.7 0.7 %copy-start.1 = (s32[128]{0:T(128)S(1)}, s32[128]{0:T(128)}, u32[]{:S(2)}) copy-start(s32[128]{0:T(128)} %param.5) | copy-start | bytes 1540
  1.4 0.7 %copy-start.2 = (s32[128]{0:T(128)S(1)}, s32[128]{0:T(128)}, u32[]{:S(2)}) copy-start(s32[128]{0:T(128)} %param.6) | copy-start | bytes 1540
  5.4 5.4 %collective-permute-start = (bf16[128,256]{1,0:T(8,128)(2,1)S(1)}, bf16[128,256]{1,0:T(8,128)(2,1)S(1)}, u32[]{:S(2)}, u32[]{:S(2)}) collective-permute-start(bf16[128,256]{1,0:T(8,128)(2,1)S(1)} %get-tuple-element.9), channel_id=1, source_target_pairs={{0,1},{1,0},{2,3},{3,2},{4,5},{5,4},{6,7},{7,6},{8,9},{9,8},{10,11... | collective-permute-start | bytes 196616 | tf_op jit(solution)/shard_map/ppermute | solution.py:31
  10.8 5.3 %collective-permute-start.1 = (bf16[128,256]{1,0:T(8,128)(2,1)S(1)}, bf16[128,256]{1,0:T(8,128)(2,1)S(1)}, u32[]{:S(2)}, u32[]{:S(2)}) collective-permute-start(bf16[128,256]{1,0:T(8,128)(2,1)S(1)} %add.15), channel_id=1, source_target_pairs={{0,2},{1,3},{2,0},{3,1},{4,6},{5,7},{6,4},{7,5},{8,10},{9,11},{10,... | collective-permute-start | bytes 196616 | tf_op jit(solution)/shard_map/ppermute | solution.py:31
  20.7 7.7 %collective-permute-start.10 = (f32[32,256]{1,0:T(8,128)S(1)}, f32[32,256]{1,0:T(8,128)S(1)}, u32[]{:S(2)}, u32[]{:S(2)}) collective-permute-start(f32[32,256]{1,0:T(8,128)S(1)} %get-tuple-element.15), channel_id=1, source_target_pairs={{0,3},{1,2},{2,1},{3,0},{4,7},{5,6},{6,5},{7,4},{8,11},{9,10},{10,... | collective-permute-start | bytes 98312 | tf_op jit(solution)/shard_map/ppermute | solution.py:31
  25.3 3.9 %collective-permute-start.8 = (f32[32,256]{1,0:T(8,128)S(1)}, f32[32,256]{1,0:T(8,128)S(1)}, u32[]{:S(2)}, u32[]{:S(2)}) collective-permute-start(f32[32,256]{1,0:T(8,128)S(1)} %get-tuple-element.13), channel_id=1, source_target_pairs={{0,1},{1,0},{2,3},{3,2},{4,5},{5,4},{6,7},{7,6},{8,9},{9,8},{10,11... | collective-permute-start | bytes 98312 | tf_op jit(solution)/shard_map/ppermute | solution.py:31
  25.3 5.4 %collective-permute-start.9 = (f32[32,256]{1,0:T(8,128)S(1)}, f32[32,256]{1,0:T(8,128)S(1)}, u32[]{:S(2)}, u32[]{:S(2)}) collective-permute-start(f32[32,256]{1,0:T(8,128)S(1)} %get-tuple-element.14), channel_id=1, source_target_pairs={{0,2},{1,3},{2,0},{3,1},{4,6},{5,7},{6,4},{7,5},{8,10},{9,11},{10,... | collective-permute-start | bytes 98312 | tf_op jit(solution)/shard_map/ppermute | solution.py:31
  25.9 1.5 %collective-permute-start.5 = (f32[8,128]{1,0:T(8,128)S(1)}, f32[8,128]{1,0:T(8,128)S(1)}, u32[]{:S(2)}, u32[]{:S(2)}) collective-permute-start(f32[8,128]{1,0:T(8,128)S(1)} %get-tuple-element.11.refs_4_), channel_id=1, source_target_pairs={{0,4},{4,0},{8,12},{12,8},{1,5},{5,1},{9,13},{13,9},{2,6},{6,2},{1... | collective-permute-start | bytes 12296 | tf_op jit(solution)/shard_map/ppermute | solution.py:31
  25.9 5.4 %collective-permute-start.6 = (f32[8,128]{1,0:T(8,128)S(1)}, f32[8,128]{1,0:T(8,128)S(1)}, u32[]{:S(2)}, u32[]{:S(2)}) collective-permute-start(f32[8,128]{1,0:T(8,128)S(1)} %get-tuple-element.11.refs_4_), channel_id=1, source_target_pairs={{0,8},{4,12},{8,0},{12,4},{1,9},{5,13},{9,1},{13,5},{2,10},{6,14},... | collective-permute-start | bytes 12296 | tf_op jit(solution)/shard_map/ppermute | solution.py:31
  27.4 3.9 %collective-permute-start.7 = (f32[8,128]{1,0:T(8,128)S(1)}, f32[8,128]{1,0:T(8,128)S(1)}, u32[]{:S(2)}, u32[]{:S(2)}) collective-permute-start(f32[8,128]{1,0:T(8,128)S(1)} %get-tuple-element.11.refs_4_), channel_id=1, source_target_pairs={{0,12},{4,8},{8,4},{12,0},{1,13},{5,9},{9,5},{13,1},{2,14},{6,10},... | collective-permute-start | bytes 12296 | tf_op jit(solution)/shard_map/ppermute | solution.py:31
  28.4 3.0 %collective-permute-start.2 = (bf16[128,256]{1,0:T(8,128)(2,1)S(1)}, bf16[128,256]{1,0:T(8,128)(2,1)S(1)}, u32[]{:S(2)}, u32[]{:S(2)}) collective-permute-start(bf16[128,256]{1,0:T(8,128)(2,1)S(1)} %add.16.refs_0_), channel_id=1, source_target_pairs={{0,4},{4,0},{8,12},{12,8},{1,5},{5,1},{9,13},{13,9},{2,6},{6,2},{1... | collective-permute-start | bytes 196616 | tf_op jit(solution)/shard_map/ppermute | solution.py:31
  29.2 4.3 %collective-permute-start.3 = (bf16[128,256]{1,0:T(8,128)(2,1)S(1)}, bf16[128,256]{1,0:T(8,128)(2,1)S(1)}, u32[]{:S(2)}, u32[]{:S(2)}) collective-permute-start(bf16[128,256]{1,0:T(8,128)(2,1)S(1)} %add.16.refs_0_), channel_id=1, source_target_pairs={{0,8},{4,12},{8,0},{12,4},{1,9},{5,13},{9,1},{13,5},{2,10},{6,14},... | collective-permute-start | bytes 196616 | tf_op jit(solution)/shard_map/ppermute | solution.py:31
  30.7 4.1 %collective-permute-start.4 = (bf16[128,256]{1,0:T(8,128)(2,1)S(1)}, bf16[128,256]{1,0:T(8,128)(2,1)S(1)}, u32[]{:S(2)}, u32[]{:S(2)}) collective-permute-start(bf16[128,256]{1,0:T(8,128)(2,1)S(1)} %add.16.refs_0_), channel_id=1, source_target_pairs={{0,12},{4,8},{8,4},{12,0},{1,13},{5,9},{9,5},{13,1},{2,14},{6,10},... | collective-permute-start | bytes 196616 | tf_op jit(solution)/shard_map/ppermute | solution.py:31
